TPU v7x, 32 devices: a whole 2x2x4 slice. The times are simulated.
32 devices in a mesh: pair: 4 (over z), virt: 8 (over y, x, core).
Axes of the slice: x: 2, y: 2, z: 4, core: 2. Of those that a mesh axis runs over, the one named last changes fastest.
Arguments:
- amplitudes: bfloat16 [4, 8, 2048, 2048], P('pair', None, 'virt'), may hold values from -6 to 6
- factor: bfloat16 [8192, 1024], P('virt'), may hold values from -0.125 to 0.125
- home: int32 [128], replicated, may hold values from 0 to 127, as said below
- domains: int32 [4, 32], P('pair'), may hold values from 0 to 127, as said below
- coupling: bfloat16 [1024, 1024], P('virt'), may hold values from -6 to 6
- hole_weight: bfloat16 [4, 3, 1024], P('pair', None, 'virt'), may hold values from -3 to 3
- virt_energy: float32 [8192], replicated, may hold values from 0.1 to 1
- occ_i: float32 [8], replicated, may hold values from -0.6 to -0.1
- occ_j: float32 [4], P('pair'), may hold values from -0.6 to -0.1
Outputs:
- residual: float32 [4, 8, 2048, 2048], P('pair', None, 'virt')
Inputs may be any that keep to these rules, and one draw needn't show every extreme that they name: `home`: a permutation of the virtual tiles; device k of virt stores the factor rows of slots k * 16 to (k + 1) * 16 - 1. `domains`: each row lists 32 distinct virtual tiles; at most 4 of a row's tiles are stored on any one device of virt, and in every row some device stores exactly 4 of them.
All inputs are finite; a program needn't handle non-finite values.
Results may differ from a plain program's by a relative error of at most 0.0033.
Values may be sent and summed in bfloat16 or wider, within the bound.
No kernel may reach another device: no remote copies, remote signals or barrier semaphores. Data moves between devices by JAX's collectives and lax.ppermute only.
A program may use at most 128 MiB of HBM per device.

v0:
```python
import jax
import jax.numpy as jnp
from jax import lax
from jax.sharding import PartitionSpec as P

TILE = 64
CAP = 4


def with_halo(array, sides, width):
    for axis, dim in sides:
        peers, length = (lax.axis_size(axis), array.shape[dim])
        up = [(i, (i + 1) % peers) for i in range(peers - 1)]
        down = [(j, i) for i, j in up]
        last = lax.slice_in_dim(array, length - width, length, axis=dim)
        first = lax.slice_in_dim(array, 0, width, axis=dim)
        before = lax.ppermute(last, axis, up)
        after = lax.ppermute(first, axis, down)
        array = jnp.concatenate([before, array, after], axis=dim)
    return array


def on_device(amplitudes, factor, home, domains, coupling, hole_weight, virt_energy, occ_i, occ_j):
    factor_cols = factor.shape[1]
    per_device = factor.shape[0] // TILE
    tile_total = home.shape[0]
    domain_entry_row = domains[0]
    slot_of = jnp.sum(
        jnp.where(
            home[None, :] == domain_entry_row[:, None],
            jnp.arange(tile_total, dtype=jnp.int32)[None, :],
            0,
        ),
        axis=1,
    )
    holder = slot_of // per_device
    offset = slot_of % per_device
    domain_len = domain_entry_row.shape[0]
    earlier = jnp.arange(domain_len)[None, :] < jnp.arange(domain_len)[:, None]
    same_holder = holder[None, :] == holder[:, None]
    position = jnp.sum((earlier & same_holder).astype(jnp.int32), axis=1)
    locally_owned = holder == lax.axis_index("virt")
    chosen = locally_owned[None, :] & (
        position[None, :] == jnp.arange(CAP, dtype=jnp.int32)[:, None]
    )
    local_slot = jnp.sum(jnp.where(chosen, offset[None, :], 0), axis=1)
    filled = jnp.any(chosen, axis=1)
    own_tiles = factor.reshape(per_device, TILE, factor_cols)
    outgoing = jnp.where(filled[:, None, None], own_tiles[local_slot], jnp.zeros((), factor.dtype))
    arrived = lax.all_gather(outgoing, "virt", axis=0, tiled=True)
    domain_coefficient = arrived[holder * CAP + position].reshape(-1, factor_cols)
    cluster_amplitude = amplitudes[0]
    half = jnp.einsum(
        "hjm,mf->hfj", cluster_amplitude, domain_coefficient, preferred_element_type=jnp.float32
    ).astype(jnp.bfloat16)
    projected = jnp.einsum(
        "iqd,dp->iqp",
        lax.all_to_all(half, "virt", split_axis=1, concat_axis=2, tiled=True),
        domain_coefficient,
        preferred_element_type=jnp.float32,
    ).astype(jnp.bfloat16)
    neighbours = with_halo(projected[None], (("pair", 0),), 1)
    weights = hole_weight[0].astype(jnp.float32)
    hole = (
        weights[0][None, :, None] * neighbours[0].astype(jnp.float32)
        + weights[1][None, :, None] * neighbours[1].astype(jnp.float32)
        + weights[2][None, :, None] * neighbours[2].astype(jnp.float32)
    )
    dressed = (coupling.astype(jnp.float32)[None] * projected.astype(jnp.float32) + hole).astype(
        jnp.bfloat16
    )
    back = jnp.einsum(
        "iqp,ap->iqa", dressed, domain_coefficient, preferred_element_type=jnp.float32
    ).astype(jnp.bfloat16)
    ladder = jnp.einsum(
        "iqa,bq->iab",
        lax.all_to_all(back, "virt", split_axis=2, concat_axis=1, tiled=True),
        domain_coefficient,
        preferred_element_type=jnp.float32,
    )
    rows_here = cluster_amplitude.shape[1]
    domain_width = cluster_amplitude.shape[2]
    spots = jnp.arange(domain_width, dtype=jnp.int32)
    orbitals = domain_entry_row[spots // TILE] * TILE + spots % TILE
    col_energy = virt_energy[orbitals]
    row_energy = lax.dynamic_slice_in_dim(col_energy, lax.axis_index("virt") * rows_here, rows_here)
    shift = row_energy[None, :, None] + col_energy[None, None, :] - occ_i[:, None, None] - occ_j[0]
    return (ladder + shift * cluster_amplitude.astype(jnp.float32))[None]


def solution(mesh):
    placed = (
        P("pair", None, "virt", None),
        P("virt", None),
        P(),
        P("pair", None),
        P("virt", None),
        P("pair", None, "virt"),
        P(),
        P(),
        P("pair"),
    )
    return jax.shard_map(
        on_device,
        mesh=mesh,
        in_specs=placed,
        out_specs=P("pair", None, "virt", None),
        check_vma=False,
    )
```

profile of v0, /device:TPU:0, one launch (start us, length us, event | category | flops | bytes accessed | tf_op | source)
XLA Modules:
  0.0 298.6 jit_solution(13571353873547823776)
XLA Ops:
  6.5 0.0 copy-start
  6.5 0.0 all-gather.2.cloned.1.call-start
  6.5 1.0 select_reduce_fusion
  7.6 0.2 convert_reduce_fusion
  7.8 0.1 fusion.18
  7.9 0.1 select_reduce_fusion.1
  8.0 0.1 copy-done
  8.2 0.6 gather_fusion
  8.7 0.9 broadcast_select_fusion
  9.6 0.0 all-gather.2.cloned.1.call-update
  9.7 39.4 %all-gather.2.cloned.1.call-done = bf16[32,64,1024]{2,1,0:T(8,128)(2,1)} async-done(((bf16[4,64,1024]{2,1,0:T(8,128)(2,1)}), bf16[32,64,1024]{2,1,0:T(8,128)(2,1)}) %all-gather.2.cloned.1.call-update) | async-done | bytes 4194320 | tf_op jit(solution)/shard_map/all_gather | solution.py:50
  49.1 4.9 %gather_fusion.1 = bf16[32,64,1024]{2,1,0:T(8,128)(2,1)} fusion(bf16[32,64,1024]{2,1,0:T(8,128)(2,1)} %all-gather.2.cloned.1.call-done, s32[1024]{0:T(1024)S(1)} %pad_clamp_fusion), kind=kCustom, calls=%fused_computation.1 | custom fusion | bytes 8388736 | tf_op jit(solution)/shard_map/gather | solution.py:51
  54.1 12.6 %convert_bitcast_fusion = bf16[8,1024,256]{2,1,0:T(8,128)(2,1)S(1)} fusion(bf16[2048,1024,1]{1,0,2:T(8,128)(2,1)} %bitcast.116, bf16[1,8,256,2048]{3,2,1,0:T(8,128)(2,1)} %param.9), kind=kOutput, calls=%fused_computation.16 | convolution fusion | flops 8592031744 | bytes 16777216 | tf_op jit(solution)/shard_map/hjm,mf->hfj/dot_general | solution.py:53
  66.7 2.4 copy.22
  69.1 51.6 %all_to_all.36 = bf16[8,1024,256]{2,0,1:T(8,128)(2,1)S(1)} all-to-all(bf16[8,1024,256]{2,0,1:T(8,128)(2,1)S(1)} %copy.22), channel_id=1, replica_groups=mesh['pair'=4,'virt'=8] {'virt'}, dimensions={1} | all-to-all | bytes 8388608 | tf_op jit(solution)/shard_map/all_to_all | solution.py:58
  120.7 4.4 %copy.31 = bf16[8,8,128,256]{3,1,2,0:T(8,128)(2,1)} copy(bf16[8,8,128,256]{3,0,2,1:T(8,128)(2,1)S(1)} %bitcast.113) | data formatting | bytes 8388608 | tf_op jit(solution)/shard_map/all_to_all | solution.py:58
  125.1 7.4 %all_to_all.29 = bf16[8,128,2048]{2,1,0:T(8,128)(2,1)} reshape(bf16[8,128,8,256]{3,2,1,0:T(8,128)(2,1)} %bitcast.114) | data formatting | bytes 8388608 | tf_op jit(solution)/shard_map/all_to_all | solution.py:58
  132.5 0.0 copy-start.6
  132.5 0.0 copy-start.5
  132.5 0.0 copy-start.3
  132.5 8.1 %convolution_convert_fusion.1 = bf16[8,128,1024]{2,1,0:T(8,128)(2,1)S(1)} fusion(bf16[8,128,2048]{2,1,0:T(8,128)(2,1)} %all_to_all.29, bf16[2048,1024,1]{1,0,2:T(8,128)(2,1)} %bitcast.117), kind=kOutput, calls=%fused_computation.24 | convolution fusion | flops 4296015872 | bytes 10485760 | tf_op jit(solution)/shard_map/iqd,dp->iqp/dot_general | solution.py:56
  140.6 1.3 collective-permute-start.1
  141.9 4.7 %collective-permute-start = (bf16[1,8,128,1024]{3,2,1,0:T(8,128)(2,1)S(1)}, bf16[1,8,128,1024]{3,2,1,0:T(8,128)(2,1)S(1)}, u32[]{:S(2)}, u32[]{:S(2)}) collective-permute-start(bf16[1,8,128,1024]{3,2,1,0:T(8,128)(2,1)S(1)} %bitcast.125), channel_id=1, source_target_pairs={{0,8},{8,16},{16,24},{1,9},{9,17},{17,25},{2,10},{10,18},{18,26},{... | collective-permute-start | bytes 6291464 | tf_op jit(solution)/shard_map/ppermute | solution.py:17
  146.6 0.0 copy-done.6
  146.6 0.0 copy-done.5
  146.7 42.6 %collective-permute-done.1 = bf16[1,8,128,1024]{3,2,1,0:T(8,128)(2,1)S(1)} collective-permute-done((bf16[1,8,128,1024]{3,2,1,0:T(8,128)(2,1)S(1)}, bf16[1,8,128,1024]{3,2,1,0:T(8,128)(2,1)S(1)}, u32[]{:S(2)}, u32[]{:S(2)}) %collective-permute-start.1) | collective-permute-done | bytes 2097184 | tf_op jit(solution)/shard_map/ppermute | solution.py:18
  189.3 1.2 collective-permute-done
  190.5 0.0 copy-done.3
  190.5 7.3 %convolution_convert_fusion = bf16[8,128,2048]{2,1,0:T(8,128)(2,1)} fusion(bf16[2048,1024,1]{1,0,2:T(8,128)(2,1)S(1)} %bitcast.119, bf16[8,128,1024]{2,1,0:T(8,128)(2,1)S(1)} %convolution_convert_fusion.1, bf16[1,8,128,1024]{3,2,1,0:T(8,128)(2,1)S(1)} %collective-permute-done.1, bf16[1,8,128,1024]{3,2,1,0:T(8,128)(2,1)S(1)} %collective-permute-done, ...), kind=kOutput, calls=%fused_computation.17 | convolution fusion | flops 4308598784 | bytes 15205888 | tf_op jit(solution)/shard_map/iqp,ap->iqa/dot_general | solution.py:72
  197.7 6.7 %copy.24 = bf16[8,128,2048]{1,0,2:T(8,128)(2,1)} copy(bf16[8,128,2048]{2,1,0:T(8,128)(2,1)} %convolution_convert_fusion) | data formatting | bytes 8388608 | tf_op jit(solution)/shard_map/convert_element_type | solution.py:74
  204.4 4.7 %all-to-all-start.1 = ((bf16[8,128,2048]{1,0,2:T(8,128)(2,1)}), bf16[8,128,2048]{1,0,2:T(8,128)(2,1)}, u32[]{:S(2)}, u32[]{:S(2)}) async-start(bf16[8,128,2048]{1,0,2:T(8,128)(2,1)} %copy.24), calls=%async_computation.1 | async-start | bytes 8388608 | tf_op jit(solution)/shard_map/all_to_all | solution.py:77
  209.8 0.1 compare_reduce_fusion.24
  210.9 0.3 compare_reduce_fusion
  211.1 0.0 copy-done.4
  211.1 0.7 fusion.22
  211.8 0.7 fusion.21
  212.6 4.3 %compare_select_fusion.2 = s32[2048,1]{0,1:T(1,128)S(1)} fusion(s32[]{:T(128)} %bitcast.47, s32[]{:T(128)} %bitcast.48, s32[]{:T(128)} %bitcast.49, s32[]{:T(128)} %bitcast.50, s32[]{:T(128)} %bitcast.51, s32[]{:T(128)} %bitcast.53, s32[]{:T(128)} %bitcast.52), kind=kLoop, calls=%fused_computation.54 | loop fusion | flops 47104 | bytes 8220 | tf_op jit(solution)/shard_map/gather | solution.py:84
  216.8 15.7 %select_multiply_fusion = s32[2048]{0:T(1024)S(1)} fusion(pred[2048]{0:T(1024)(128)(4,1)S(1)} %compare_reduce_fusion, pred[2048]{0:T(1024)(128)(4,1)S(1)} %compare_reduce_fusion.1, pred[2048]{0:T(1024)(128)(4,1)S(1)} %compare_reduce_fusion.2, pred[2048]{0:T(1024)(128)(4,1)S(1)} %compare_reduce_fusion.3, pred[2048]{0:T(1024)(128)(4,1)S(1)} %compare_reduce_fusion.4, ...), kind=kLoop, calls=%fused_computation.70 | loop fusion | flops 53248 | bytes 67684 | tf_op jit(solution)/shard_map/mul | solution.py:84
  232.6 0.0 copy-done.2
  232.6 11.8 %gather_fusion.2 = f32[2048]{0:T(1024)S(1)} fusion(f32[8192]{0:T(1024)S(1)} %copy-done.2, s32[2048]{0:T(1024)S(1)} %broadcast_clamp_fusion), kind=kCustom, calls=%fused_computation.2 | custom fusion | bytes 24576 | tf_op jit(solution)/shard_map/gather | solution.py:85
  244.4 0.1 dynamic_slice.3
  244.4 1.6 broadcast_add_fusion
  246.0 12.2 %all-to-all-done.1 = bf16[8,128,2048]{1,0,2:T(8,128)(2,1)} async-done(((bf16[8,128,2048]{1,0,2:T(8,128)(2,1)}), bf16[8,128,2048]{1,0,2:T(8,128)(2,1)}, u32[]{:S(2)}, u32[]{:S(2)}) %all-to-all-start.1) | async-done | bytes 4194336 | tf_op jit(solution)/shard_map/all_to_all | solution.py:77
  258.2 6.9 %copy.30 = bf16[8,128,8,256]{1,2,3,0:T(8,128)(2,1)} copy(bf16[8,128,8,256]{1,0,3,2:T(8,128)(2,1)} %bitcast.20) | data formatting | bytes 8388608 | tf_op jit(solution)/shard_map/all_to_all | solution.py:77
  265.1 7.3 %all_to_all.33 = bf16[8,1024,256]{1,2,0:T(8,128)(2,1)} reshape(bf16[8,8,128,256]{2,1,3,0:T(8,128)(2,1)} %bitcast.115) | data formatting | bytes 8388608 | tf_op jit(solution)/shard_map/all_to_all | solution.py:77
  272.4 0.0 copy-done.7
  272.4 19.3 %add_bitcast_fusion = f32[1,8,256,2048]{3,2,1,0:T(8,128)} fusion(bf16[1,8,256,2048]{3,2,1,0:T(8,128)(2,1)} %param.9, f32[]{:T(128)} %bitcast.111, f32[8]{0:T(128)S(1)} %copy-done.7, f32[256,2048]{1,0:T(8,128)} %broadcast_add_fusion, bf16[8,1024,256]{1,2,0:T(8,128)(2,1)} %all_to_all.33, bf16[2048,1024,1]{1,0,2:T(8,128)(2,1)} %bitcast.118), kind=kOutput, calls=%fused_computation.3 | convolution fusion | flops 8610906112 | bytes 35651620 | tf_op jit(solution)/shard_map/iqa,bq->iab/dot_general | solution.py:75
  291.7 0.0 copy-done.1
  (38 shorter events, 1.2 us)
Async XLA Ops:
  6.5 1.6 copy-start
  6.5 42.6 %all-gather.2.cloned.1.call-start = ((), (), s32[]{:S(2)}) async-start(), calls=%async_computation.2 | async-start | bytes 4718592 | tf_op jit(solution)/shard_map/all_gather | solution.py:50
  132.5 14.1 %copy-start.6 = (bf16[1,3,128]{2,1,0:T(4,128)(2,1)S(1)}, bf16[1,3,128]{2,1,0:T(4,128)(2,1)}, u32[]{:S(2)}) copy-start(bf16[1,3,128]{2,1,0:T(4,128)(2,1)} %param.14) | copy-start | bytes 2308
  132.5 14.1 %copy-start.5 = (bf16[128,1024]{1,0:T(8,128)(2,1)S(1)}, bf16[128,1024]{1,0:T(8,128)(2,1)}, u32[]{:S(2)}) copy-start(bf16[128,1024]{1,0:T(8,128)(2,1)} %param.13) | copy-start | bytes 786436
  132.5 58.0 %copy-start.3 = (bf16[32,64,1024]{2,1,0:T(8,128)(2,1)S(1)}, bf16[32,64,1024]{2,1,0:T(8,128)(2,1)}, u32[]{:S(2)}) copy-start(bf16[32,64,1024]{2,1,0:T(8,128)(2,1)} %gather_fusion.1) | copy-start | bytes 12582916
  140.6 48.7 %collective-permute-start.1 = (bf16[1,8,128,1024]{3,2,1,0:T(8,128)(2,1)S(1)}, bf16[1,8,128,1024]{3,2,1,0:T(8,128)(2,1)S(1)}, u32[]{:S(2)}, u32[]{:S(2)}) collective-permute-start(bf16[1,8,128,1024]{3,2,1,0:T(8,128)(2,1)S(1)} %bitcast.124), channel_id=1, source_target_pairs={{8,0},{16,8},{24,16},{9,1},{17,9},{25,17},{10,2},{18,10},{26,18},{... | collective-permute-start | bytes 6291464 | tf_op jit(solution)/shard_map/ppermute | solution.py:18
  141.9 48.6 %collective-permute-start = (bf16[1,8,128,1024]{3,2,1,0:T(8,128)(2,1)S(1)}, bf16[1,8,128,1024]{3,2,1,0:T(8,128)(2,1)S(1)}, u32[]{:S(2)}, u32[]{:S(2)}) collective-permute-start(bf16[1,8,128,1024]{3,2,1,0:T(8,128)(2,1)S(1)} %bitcast.125), channel_id=1, source_target_pairs={{0,8},{8,16},{16,24},{1,9},{9,17},{17,25},{2,10},{10,18},{18,26},{... | collective-permute-start | bytes 6291464 | tf_op jit(solution)/shard_map/ppermute | solution.py:17
  204.4 6.7 %copy-start.4 = (s32[1,32]{1,0:T(1,128)S(1)}, s32[1,32]{1,0:T(1,128)}, u32[]{:S(2)}) copy-start(s32[1,32]{1,0:T(1,128)} %param.12) | copy-start | bytes 388
  204.4 28.1 %copy-start.2 = (f32[8192]{0:T(1024)S(1)}, f32[8192]{0:T(1024)}, u32[]{:S(2)}) copy-start(f32[8192]{0:T(1024)} %param.15) | copy-start | bytes 98308
  204.4 53.8 %all-to-all-start.1 = ((bf16[8,128,2048]{1,0,2:T(8,128)(2,1)}), bf16[8,128,2048]{1,0,2:T(8,128)(2,1)}, u32[]{:S(2)}, u32[]{:S(2)}) async-start(bf16[8,128,2048]{1,0,2:T(8,128)(2,1)} %copy.24), calls=%async_computation.1 | async-start | bytes 8388608 | tf_op jit(solution)/shard_map/all_to_all | solution.py:77
  265.1 7.3 %copy-start.7 = (f32[8]{0:T(128)S(1)}, f32[8]{0:T(128)}, u32[]{:S(2)}) copy-start(f32[8]{0:T(128)} %param.16) | copy-start | bytes 100
  272.4 19.3 %copy-start.1 = (bf16[1024,1024]{1,0:T(8,128)(2,1)S(1)}, bf16[1024,1024]{1,0:T(8,128)(2,1)}, u32[]{:S(2)}) copy-start(bf16[1024,1024]{1,0:T(8,128)(2,1)} %param.10) | copy-start | bytes 6291460
Sparse Core Ops, SparseCore 0:
  9.8 39.2 all-gather.1
where the time goes:
time: 300 us; the launch traced here: 299 us
  waiting for transfers between devices  95.5 us (32%)
  local copies, waits for them, and re-layouts  54.1 us (18%)
  blocking collectives  51.6 us (17%)
  matrix products  47.2 us (16%)
  other arithmetic  25.3 us (8%)
  between operations  14.2 us (5%)
  starting transfers between devices  10.7 us (4%)
    all_to_all x1, blocking collectives, on_device(): lax.all_to_all(half, 'virt', split_axis=1, concat_axis=2, tiled=True)  51.6 us
    ppermute x1, waiting for transfers between devices, with_halo(): after = lax.ppermute(first, axis, down)  42.6 us
    all_gather x1, waiting for transfers between devices, on_device(): arrived = lax.all_gather(outgoing, 'virt', axis=0, tiled=True)  39.4 us
    dot_general x1, matrix products, on_device(): jnp.einsum('iqa,bq->iab', lax.all_to_all(back, 'virt', split_axis=2, conc...  19.3 us
    mul x1, other arithmetic, on_device(): orbitals = domain_entry_row[spots // TILE] * TILE + spots % TILE  15.7 us
    all_to_all x2, local copies, waits for them, and re-layouts, on_device(): lax.all_to_all(back, 'virt', split_axis=2, concat_axis=1, tiled=True)  14.2 us
    dot_general x1, matrix products, on_device(): jnp.einsum('hjm,mf->hfj', cluster_amplitude, domain_coefficient, preferre...  12.6 us
    all_to_all x1, waiting for transfers between devices, on_device(): lax.all_to_all(back, 'virt', split_axis=2, concat_axis=1, tiled=True)  12.2 us
  transfers between devices with their start and end apart: 4, of which 4 were waited for; matrix products, arithmetic and copies ran while one was open for 12% of the time, Pallas kernels for 0%

commit v1 on v0

--- a/solution.py
+++ b/solution.py
@@ -74,7 +74,10 @@
     ).astype(jnp.bfloat16)
     ladder = jnp.einsum(
         "iqa,bq->iab",
-        lax.all_to_all(back, "virt", split_axis=2, concat_axis=1, tiled=True),
+        jnp.concatenate(
+            lax.all_to_all(jnp.stack(jnp.split(back, lax.axis_size("virt"), axis=2)), "virt", 0, 0),
+            axis=1,
+        ),
         domain_coefficient,
         preferred_element_type=jnp.float32,
     )

time: 300 us -> 288 us (0.960)
  local copies, waits for them, and re-layouts: 54.1 us -> 44.4 us
    all_to_all x2 -> x0, local copies, waits for them, and re-layouts: 14.2 us -> none  [on_device(): lax.all_to_all(back, 'virt', split_axis=2, concat_axis=1, tiled=True)]
    unnamed x16 -> x27, local copies, waits for them, and re-layouts: 0.17 us -> 7.84 us
    convert_element_type x1 -> x0, local copies, waits for them, and re-layouts: 6.67 us -> none  [on_device(): back = jnp.einsum('iqp,ap->iqa', dressed, domain_coefficient, preferred_e...]
  transfers between devices with their start and end apart: 4 -> 4, of which waited for: 4 -> 4; matrix products, arithmetic and copies ran while one was open for 12% -> 13% of each run, Pallas kernels for 0% -> 0%
where the time goes in v1:
time: 288 us; the launch traced here: 287 us
  waiting for transfers between devices  95.6 us (33%)
  blocking collectives  51.6 us (18%)
  matrix products  45.4 us (16%)
  local copies, waits for them, and re-layouts  44.4 us (15%)
  other arithmetic  25.2 us (9%)
  between operations  14.3 us (5%)
  starting transfers between devices  10.6 us (4%)
    all_to_all x1, blocking collectives, on_device(): lax.all_to_all(half, 'virt', split_axis=1, concat_axis=2, tiled=True)  51.6 us
    ppermute x1, waiting for transfers between devices, with_halo(): after = lax.ppermute(first, axis, down)  42.6 us
    all_gather x1, waiting for transfers between devices, on_device(): arrived = lax.all_gather(outgoing, 'virt', axis=0, tiled=True)  39.4 us
    dot_general x1, matrix products, on_device(): jnp.einsum('iqa,bq->iab', jnp.concatenate(lax.all_to_all(jnp.stack(jnp.sp...  18.8 us
    mul x1, other arithmetic, on_device(): orbitals = domain_entry_row[spots // TILE] * TILE + spots % TILE  15.4 us
    dot_general x1, matrix products, on_device(): jnp.einsum('hjm,mf->hfj', cluster_amplitude, domain_coefficient, preferre...  12.6 us
    all_to_all x1, waiting for transfers between devices, on_device(): lax.all_to_all(jnp.stack(jnp.split(back, lax.axis_size('virt'), axis=2)),...  12.3 us
    gather x1, local copies, waits for them, and re-layouts, on_device(): col_energy = virt_energy[orbitals]  11.8 us
  transfers between devices with their start and end apart: 4, of which 4 were waited for; matrix products, arithmetic and copies ran while one was open for 13% of the time, Pallas kernels for 0%

profile of v1, /device:TPU:0, one launch (start us, length us, event | category | flops | bytes accessed | tf_op | source)
XLA Modules:
  0.0 287.0 jit_solution(10474148213058548309)
XLA Ops:
  6.5 0.0 copy-start
  6.5 0.0 all-gather.2.cloned.1.call-start
  6.5 1.0 select_reduce_fusion
  7.6 0.2 convert_reduce_fusion
  7.8 0.1 fusion.26
  7.9 0.1 select_reduce_fusion.1
  8.0 0.1 copy-done
  8.2 0.6 gather_fusion
  8.7 0.9 broadcast_select_fusion
  9.6 0.0 all-gather.2.cloned.1.call-update
  9.7 39.4 %all-gather.2.cloned.1.call-done = bf16[32,64,1024]{2,1,0:T(8,128)(2,1)} async-done(((bf16[4,64,1024]{2,1,0:T(8,128)(2,1)}), bf16[32,64,1024]{2,1,0:T(8,128)(2,1)}) %all-gather.2.cloned.1.call-update) | async-done | bytes 4194320 | tf_op jit(solution)/shard_map/all_gather | solution.py:50
  49.1 5.0 %gather_fusion.1 = bf16[32,64,1024]{2,1,0:T(8,128)(2,1)} fusion(bf16[32,64,1024]{2,1,0:T(8,128)(2,1)} %all-gather.2.cloned.1.call-done, s32[1024]{0:T(1024)S(1)} %pad_clamp_fusion), kind=kCustom, calls=%fused_computation.1 | custom fusion | bytes 8388736 | tf_op jit(solution)/shard_map/gather | solution.py:51
  54.1 12.6 %convert_bitcast_fusion = bf16[8,1024,256]{2,1,0:T(8,128)(2,1)S(1)} fusion(bf16[2048,1024,1]{1,0,2:T(8,128)(2,1)} %bitcast.141, bf16[1,8,256,2048]{3,2,1,0:T(8,128)(2,1)} %param.9), kind=kOutput, calls=%fused_computation.15 | convolution fusion | flops 8592031744 | bytes 16777216 | tf_op jit(solution)/shard_map/hjm,mf->hfj/dot_general | solution.py:53
  66.7 2.4 copy.22
  69.2 51.6 %all_to_all.23 = bf16[8,1024,256]{2,0,1:T(8,128)(2,1)S(1)} all-to-all(bf16[8,1024,256]{2,0,1:T(8,128)(2,1)S(1)} %copy.22), channel_id=1, replica_groups=mesh['pair'=4,'virt'=8] {'virt'}, dimensions={1} | all-to-all | bytes 8388608 | tf_op jit(solution)/shard_map/all_to_all | solution.py:58
  120.7 4.3 %copy.30 = bf16[8,8,128,256]{3,1,2,0:T(8,128)(2,1)} copy(bf16[8,8,128,256]{3,0,2,1:T(8,128)(2,1)S(1)} %bitcast.139) | data formatting | bytes 8388608 | tf_op jit(solution)/shard_map/all_to_all | solution.py:58
  125.1 7.4 %all_to_all.19 = bf16[8,128,2048]{2,1,0:T(8,128)(2,1)} reshape(bf16[8,128,8,256]{3,2,1,0:T(8,128)(2,1)} %bitcast.140) | data formatting | bytes 8388608 | tf_op jit(solution)/shard_map/all_to_all | solution.py:58
  132.5 8.1 %convolution_convert_fusion.1 = bf16[8,128,1024]{2,1,0:T(8,128)(2,1)S(1)} fusion(bf16[8,128,2048]{2,1,0:T(8,128)(2,1)} %all_to_all.19, bf16[2048,1024,1]{1,0,2:T(8,128)(2,1)} %bitcast.142), kind=kOutput, calls=%fused_computation.23 | convolution fusion | flops 4296015872 | bytes 10485760 | tf_op jit(solution)/shard_map/iqd,dp->iqp/dot_general | solution.py:56
  140.6 1.3 collective-permute-start.1
  141.9 4.7 %collective-permute-start = (bf16[1,8,128,1024]{3,2,1,0:T(8,128)(2,1)S(1)}, bf16[1,8,128,1024]{3,2,1,0:T(8,128)(2,1)S(1)}, u32[]{:S(2)}, u32[]{:S(2)}) collective-permute-start(bf16[1,8,128,1024]{3,2,1,0:T(8,128)(2,1)S(1)} %bitcast.151), channel_id=1, source_target_pairs={{0,8},{8,16},{16,24},{1,9},{9,17},{17,25},{2,10},{10,18},{18,26},{... | collective-permute-start | bytes 6291464 | tf_op jit(solution)/shard_map/ppermute | solution.py:17
  146.6 0.0 copy-done.8
  146.7 42.6 %collective-permute-done.1 = bf16[1,8,128,1024]{3,2,1,0:T(8,128)(2,1)S(1)} collective-permute-done((bf16[1,8,128,1024]{3,2,1,0:T(8,128)(2,1)S(1)}, bf16[1,8,128,1024]{3,2,1,0:T(8,128)(2,1)S(1)}, u32[]{:S(2)}, u32[]{:S(2)}) %collective-permute-start.1) | collective-permute-done | bytes 2097184 | tf_op jit(solution)/shard_map/ppermute | solution.py:18
  189.3 1.2 collective-permute-done
  190.5 5.9 %convolution_convert_fusion = bf16[8,128,2048]{2,1,0:T(8,128)(2,1)S(1)} fusion(bf16[2048,1024,1]{1,0,2:T(8,128)(2,1)S(1)} %bitcast.143, bf16[8,128,1024]{2,1,0:T(8,128)(2,1)S(1)} %convolution_convert_fusion.1, bf16[1,8,128,1024]{3,2,1,0:T(8,128)(2,1)S(1)} %collective-permute-done.1, bf16[1,8,128,1024]{3,2,1,0:T(8,128)(2,1)S(1)} %collective-permute-done, ...), kind=kOutput, calls=%fused_computation.16 | convolution fusion | flops 4308598784 | bytes 15205888 | tf_op jit(solution)/shard_map/iqp,ap->iqa/dot_general | solution.py:72
  196.4 0.9 fusion.22
  197.3 0.9 fusion.21
  198.2 0.9 fusion.20
  199.1 0.9 fusion.19
  199.9 0.9 fusion.18
  200.8 0.9 fusion.17
  201.7 0.9 fusion.16
  202.6 0.9 fusion.15
  203.5 4.7 %all-to-all-start.1 = ((bf16[8,8,128,256]{3,2,1,0:T(8,128)(2,1)}), bf16[8,8,128,256]{3,2,1,0:T(8,128)(2,1)}, u32[]{:S(2)}, u32[]{:S(2)}) async-start(bf16[8,8,128,256]{3,2,1,0:T(8,128)(2,1)} %fusion.15), calls=%async_computation.1 | async-start | bytes 8388608 | tf_op jit(solution)/shard_map/all_to_all | solution.py:78
  208.8 0.1 compare_reduce_fusion.24
  209.9 0.3 compare_reduce_fusion
  210.2 0.0 copy-done.6
  210.2 0.7 fusion.30
  210.9 0.7 fusion.29
  211.6 4.4 %compare_select_fusion.2 = s32[2048,1]{0,1:T(1,128)S(1)} fusion(s32[]{:T(128)} %bitcast.55, s32[]{:T(128)} %bitcast.56, s32[]{:T(128)} %bitcast.57, s32[]{:T(128)} %bitcast.58, s32[]{:T(128)} %bitcast.59, s32[]{:T(128)} %bitcast.61, s32[]{:T(128)} %bitcast.60), kind=kLoop, calls=%fused_computation.69 | loop fusion | flops 47104 | bytes 8220 | tf_op jit(solution)/shard_map/gather | solution.py:87
  216.0 15.4 %select_multiply_fusion = s32[2048]{0:T(1024)S(1)} fusion(pred[2048]{0:T(1024)(128)(4,1)S(1)} %compare_reduce_fusion, pred[2048]{0:T(1024)(128)(4,1)S(1)} %compare_reduce_fusion.1, pred[2048]{0:T(1024)(128)(4,1)S(1)} %compare_reduce_fusion.2, pred[2048]{0:T(1024)(128)(4,1)S(1)} %compare_reduce_fusion.3, pred[2048]{0:T(1024)(128)(4,1)S(1)} %compare_reduce_fusion.4, ...), kind=kLoop, calls=%fused_computation.85 | loop fusion | flops 53248 | bytes 67684 | tf_op jit(solution)/shard_map/mul | solution.py:87
  231.5 11.8 %gather_fusion.2 = f32[2048]{0:T(1024)S(1)} fusion(f32[8192]{0:T(1024)S(1)} %copy-done.2, s32[2048]{0:T(1024)S(1)} %broadcast_clamp_fusion), kind=kCustom, calls=%fused_computation.2 | custom fusion | bytes 24576 | tf_op jit(solution)/shard_map/gather | solution.py:88
  243.2 0.1 dynamic_slice.3
  243.3 1.6 broadcast_add_fusion
  244.9 12.3 %all-to-all-done.1 = bf16[8,8,128,256]{3,2,1,0:T(8,128)(2,1)} async-done(((bf16[8,8,128,256]{3,2,1,0:T(8,128)(2,1)}), bf16[8,8,128,256]{3,2,1,0:T(8,128)(2,1)}, u32[]{:S(2)}, u32[]{:S(2)}) %all-to-all-start.1) | async-done | bytes 4194336 | tf_op jit(solution)/shard_map/all_to_all | solution.py:78
  257.3 2.6 copy.24
  259.9 0.8 copy-done.4
  260.7 0.7 copy-done.5
  261.4 18.8 %add_bitcast_fusion = f32[1,8,256,2048]{3,2,1,0:T(8,128)} fusion(bf16[1,8,256,2048]{3,2,1,0:T(8,128)(2,1)} %param.9, f32[]{:T(128)} %bitcast.137, f32[8]{0:T(128)S(1)} %copy-done.9, f32[256,2048]{1,0:T(8,128)S(1)} %copy-done.5, bf16[8,1024,256]{2,1,0:T(8,128)(2,1)S(1)} %bitcast.145, bf16[2048,1024,1]{1,0,2:T(8,128)(2,1)S(1)} %bitcast.144), kind=kOutput, calls=%fused_computation.3 | convolution fusion | flops 8610906112 | bytes 35651620 | tf_op jit(solution)/shard_map/iqa,bq->iab/dot_general | solution.py:75
  (48 shorter events, 1.2 us)
Async XLA Ops:
  6.5 1.6 copy-start
  6.5 42.6 %all-gather.2.cloned.1.call-start = ((), (), s32[]{:S(2)}) async-start(), calls=%async_computation.2 | async-start | bytes 4718592 | tf_op jit(solution)/shard_map/all_gather | solution.py:50
  132.5 14.1 %copy-start.8 = (bf16[1,3,128]{2,1,0:T(4,128)(2,1)S(1)}, bf16[1,3,128]{2,1,0:T(4,128)(2,1)}, u32[]{:S(2)}) copy-start(bf16[1,3,128]{2,1,0:T(4,128)(2,1)} %param.14) | copy-start | bytes 2308
  132.5 14.1 %copy-start.7 = (bf16[128,1024]{1,0:T(8,128)(2,1)S(1)}, bf16[128,1024]{1,0:T(8,128)(2,1)}, u32[]{:S(2)}) copy-start(bf16[128,1024]{1,0:T(8,128)(2,1)} %param.13) | copy-start | bytes 786436
  132.5 58.0 %copy-start.3 = (bf16[32,64,1024]{2,1,0:T(8,128)(2,1)S(1)}, bf16[32,64,1024]{2,1,0:T(8,128)(2,1)}, u32[]{:S(2)}) copy-start(bf16[32,64,1024]{2,1,0:T(8,128)(2,1)} %gather_fusion.1) | copy-start | bytes 12582916
  140.6 48.7 %collective-permute-start.1 = (bf16[1,8,128,1024]{3,2,1,0:T(8,128)(2,1)S(1)}, bf16[1,8,128,1024]{3,2,1,0:T(8,128)(2,1)S(1)}, u32[]{:S(2)}, u32[]{:S(2)}) collective-permute-start(bf16[1,8,128,1024]{3,2,1,0:T(8,128)(2,1)S(1)} %bitcast.150), channel_id=1, source_target_pairs={{8,0},{16,8},{24,16},{9,1},{17,9},{25,17},{10,2},{18,10},{26,18},{... | collective-permute-start | bytes 6291464 | tf_op jit(solution)/shard_map/ppermute | solution.py:18
  141.9 48.6 %collective-permute-start = (bf16[1,8,128,1024]{3,2,1,0:T(8,128)(2,1)S(1)}, bf16[1,8,128,1024]{3,2,1,0:T(8,128)(2,1)S(1)}, u32[]{:S(2)}, u32[]{:S(2)}) collective-permute-start(bf16[1,8,128,1024]{3,2,1,0:T(8,128)(2,1)S(1)} %bitcast.151), channel_id=1, source_target_pairs={{0,8},{8,16},{16,24},{1,9},{9,17},{17,25},{2,10},{10,18},{18,26},{... | collective-permute-start | bytes 6291464 | tf_op jit(solution)/shard_map/ppermute | solution.py:17
  203.5 6.7 %copy-start.6 = (s32[1,32]{1,0:T(1,128)S(1)}, s32[1,32]{1,0:T(1,128)}, u32[]{:S(2)}) copy-start(s32[1,32]{1,0:T(1,128)} %param.12) | copy-start | bytes 388
  203.5 28.0 %copy-start.2 = (f32[8192]{0:T(1024)S(1)}, f32[8192]{0:T(1024)}, u32[]{:S(2)}) copy-start(f32[8192]{0:T(1024)} %param.15) | copy-start | bytes 98308
  203.5 53.8 %all-to-all-start.1 = ((bf16[8,8,128,256]{3,2,1,0:T(8,128)(2,1)}), bf16[8,8,128,256]{3,2,1,0:T(8,128)(2,1)}, u32[]{:S(2)}, u32[]{:S(2)}) async-start(bf16[8,8,128,256]{3,2,1,0:T(8,128)(2,1)} %fusion.15), calls=%async_computation.1 | async-start | bytes 8388608 | tf_op jit(solution)/shard_map/all_to_all | solution.py:78
  257.2 3.4 %copy-start.4 = (bf16[32,64,1024]{2,1,0:T(8,128)(2,1)S(1)}, bf16[32,64,1024]{2,1,0:T(8,128)(2,1)}, u32[]{:S(2)}) copy-start(bf16[32,64,1024]{2,1,0:T(8,128)(2,1)} %gather_fusion.1) | copy-start | bytes 12582916
  257.2 4.1 %copy-start.5 = (f32[256,2048]{1,0:T(8,128)S(1)}, f32[256,2048]{1,0:T(8,128)}, u32[]{:S(2)}) copy-start(f32[256,2048]{1,0:T(8,128)} %broadcast_add_fusion) | copy-start | bytes 6291460
  257.3 4.1 %copy-start.9 = (f32[8]{0:T(128)S(1)}, f32[8]{0:T(128)}, u32[]{:S(2)}) copy-start(f32[8]{0:T(128)} %param.16) | copy-start | bytes 100
  261.4 18.8 %copy-start.1 = (bf16[1024,1024]{1,0:T(8,128)(2,1)S(1)}, bf16[1024,1024]{1,0:T(8,128)(2,1)}, u32[]{:S(2)}) copy-start(bf16[1024,1024]{1,0:T(8,128)(2,1)} %param.10) | copy-start | bytes 6291460
Sparse Core Ops, SparseCore 0:
  9.8 39.2 all-gather.1
